TPU v7x, 128 devices: a whole 4x4x4 slice. The times are simulated.
128 devices in a mesh: leaf: 4 (over y), row: 8 (over z, core), col: 4 (over x).
Axes of the slice: x: 4, y: 4, z: 4, core: 2. Of those that a mesh axis runs over, the one named last changes fastest.
Arguments:
- sigma_top: float32 [1024, 1024], P(('leaf', 'row'), 'col')
- panels: float32 [4, 7, 1024, 512], P('leaf', None, 'row', 'col'), may hold values from -0.1875 to 0.1875
- inverse_diag: float32 [4, 7, 512, 512], P('leaf', None, 'col')
- slot_lists: int32 [4, 6, 8], P('leaf'), may hold values from -1 to 11, as said below
- parent_links: int32 [4, 4], P('leaf'), may hold values from 1 to 2
Outputs:
- ancestor_block: float32 [4, 7, 1024, 512], P('leaf', None, 'row', 'col')
- diagonal_block: float32 [4, 7, 512, 512], P('leaf', None, None, 'col')
Inputs may be any that keep to these rules, and one draw needn't show every extreme that they name: `slot_lists`: in every row, entries 0 to 3 are 8 to 11 in order (the parent's own tiles); then come 1 to 3 distinct parent ancestor slots, below 8 for supernodes 1 and 2 and below 4 for supernodes 3 to 6; the rest are -1, so every row has padding. `parent_links`: each supernode 3 to 6 has supernode 1 or 2 as its parent. `sigma_top`: symmetric.
All inputs are finite; a program needn't handle non-finite values.
Results may differ from a plain program's by a relative error of at most 0.0001.
Values sent between devices are 32-bit elements; how exact they have to be, the bound alone decides.
A program may use at most 128 MiB of HBM per device.

v0:
```python
import jax
import jax.numpy as jnp
from jax import lax
from jax.sharding import PartitionSpec as P

TILE = 128
HIGHEST = lax.Precision.HIGHEST


def mm(a, b):
    return jnp.matmul(a, b, precision=HIGHEST, preferred_element_type=jnp.float32)


def tile_rows(matrix, index, tile):
    return lax.dynamic_slice_in_dim(matrix, index * tile, tile, 0)


def tile_cols(matrix, index, tile):
    return lax.dynamic_slice_in_dim(matrix, index * tile, tile, 1)


def scatter_factor(factor_col, slots, positions, tile):
    tiles = factor_col.reshape(slots.shape[0], tile, factor_col.shape[1])
    hits = slots[:, None] == jnp.arange(positions, dtype=slots.dtype)[None, :]
    present = jnp.any(hits, axis=0)
    source = jnp.argmax(hits, axis=0)
    moved = jnp.take(tiles, source, axis=0)
    moved = jnp.where(present[:, None, None], moved, 0.0)
    return moved.reshape(positions * tile, factor_col.shape[1])


def pick_transposed(column_block, picks, tile):
    tiles = column_block.reshape(-1, tile, tile)
    chosen = jnp.take(tiles, jnp.maximum(picks, 0), axis=0)
    chosen = jnp.where((picks >= 0)[:, None, None], chosen, 0.0)
    return jnp.transpose(chosen, (2, 0, 1)).reshape(tile, picks.shape[0] * tile)


def body(sigma_top, panels, inverse_diag, slot_lists, parent_links):
    tile = TILE
    row_count = lax.axis_size("row")
    col_count = lax.axis_size("col")
    leaf_count = lax.axis_size("leaf")
    r = lax.axis_index("row")
    c = lax.axis_index("col")
    panel = panels[0]
    inverse = inverse_diag[0]
    picks_all = slot_lists[0]
    parents = parent_links[0]
    nodes = panel.shape[0]
    width = inverse.shape[2]
    own_tiles = width // tile
    slot_count = picks_all.shape[1]
    positions = slot_count + own_tiles
    band = width // row_count
    partial_factor = mm(panel, inverse)
    factor_rows = lax.psum(partial_factor, "col")
    living = jnp.concatenate([jnp.ones((1, slot_count), jnp.bool_), picks_all >= 0], axis=0)
    live_here = jnp.take(living, r, axis=1).astype(jnp.float32)
    factor_rows = factor_rows * live_here[:, None, None]
    factor_tile = lax.dynamic_slice_in_dim(factor_rows, c * tile, tile, 2)
    factor_cols = lax.all_gather(factor_tile, "row", axis=1, tiled=True)
    inverse_band = lax.dynamic_slice_in_dim(inverse, r * band, band, 2)
    partial_gram = mm(jnp.transpose(inverse_band, (0, 2, 1)), inverse)
    gram_piece = lax.psum_scatter(partial_gram, "col", scatter_dimension=2, tiled=True)
    local_rows, local_cols = sigma_top.shape
    gathered = lax.all_gather(sigma_top, ("leaf", "row", "col"), axis=0)
    sigma = gathered.reshape(leaf_count * row_count, col_count, local_rows, local_cols)
    sigma = jnp.transpose(sigma, (0, 2, 1, 3)).reshape(
        leaf_count * row_count * local_rows, col_count * local_cols
    )

    def diag_partial(first, products):
        rows = factor_rows[first : first + products.shape[0]]
        return mm(jnp.transpose(rows, (0, 2, 1)), products)

    def reduce_and_gather(first, products):
        count = products.shape[0]
        piece = lax.psum_scatter(
            diag_partial(first, products), "row", scatter_dimension=1, tiled=True
        )
        piece = piece + gram_piece[first : first + count]
        both = jnp.concatenate([products, piece], axis=1)
        everything = lax.all_gather(both, ("row", "col"), axis=0)
        everything = everything.reshape(row_count, col_count, count, tile + band, tile)
        product_full = jnp.transpose(everything[:, :, :, :tile], (2, 0, 3, 1, 4)).reshape(
            count, row_count * tile, col_count * tile
        )
        diag_full = jnp.transpose(everything[:, :, :, tile:], (2, 0, 3, 1, 4)).reshape(
            count, row_count * band, col_count * tile
        )
        return (product_full, diag_full)

    own_row = jnp.minimum(r, own_tiles - 1)
    upper = r < own_tiles
    product_0 = mm(tile_rows(sigma, r, tile), factor_cols[0])
    product_full_0, diag_full_0 = reduce_and_gather(0, product_0[None])
    product_full_0 = product_full_0[0]
    diag_full_0 = diag_full_0[0]
    level_1 = []
    for node in (1, 2):
        slots = picks_all[node - 1]
        spread = scatter_factor(factor_cols[node], slots, positions, tile)
        top_row = jnp.concatenate(
            [
                -jnp.transpose(tile_cols(product_full_0, own_row, tile)),
                tile_rows(diag_full_0, own_row, tile),
            ],
            axis=1,
        )
        source = slots[jnp.maximum(r, own_tiles)]
        source_row = jnp.maximum(source, 0)
        low_row = jnp.concatenate(
            [tile_rows(sigma, source_row, tile), -tile_rows(product_full_0, source_row, tile)],
            axis=1,
        )
        low_row = jnp.where(source >= 0, low_row, 0.0)
        row = jnp.where(upper, top_row, low_row)
        level_1.append(mm(row, spread))
    product_1 = jnp.stack(level_1)
    product_full_1, diag_full_1 = reduce_and_gather(1, product_1)
    level_2 = []
    for node in range(3, nodes):
        slots = picks_all[node - 1]
        parent = parents[node - 3] - 1
        parent_slots = jnp.take(picks_all, parent, axis=0)
        product_p = jnp.take(product_full_1, parent, axis=0)
        diag_p = jnp.take(diag_full_1, parent, axis=0)
        spread = scatter_factor(factor_cols[node], slots, positions, tile)
        top_row = jnp.concatenate(
            [-jnp.transpose(tile_cols(product_p, own_row, tile)), tile_rows(diag_p, own_row, tile)],
            axis=1,
        )
        source = slots[jnp.maximum(r, own_tiles)]
        source_row = jnp.clip(source, 0, own_tiles - 1)
        corner = pick_transposed(
            -tile_cols(product_full_0, source_row, tile), parent_slots[own_tiles:], tile
        )
        low_row = jnp.concatenate(
            [
                tile_rows(diag_full_0, source_row, tile),
                corner,
                -tile_rows(product_p, source_row, tile),
            ],
            axis=1,
        )
        low_row = jnp.where(source >= 0, low_row, 0.0)
        row = jnp.where(upper, top_row, low_row)
        level_2.append(mm(row, spread))
    product_2 = jnp.stack(level_2)
    first_2 = 3
    count_2 = product_2.shape[0]
    gram_rows = jnp.zeros((count_2, width, tile), jnp.float32)
    gram_rows = lax.dynamic_update_slice_in_dim(
        gram_rows, gram_piece[first_2 : first_2 + count_2], r * band, 1
    )
    diag_2 = lax.psum(diag_partial(first_2, product_2) + gram_rows, "row")
    products = jnp.concatenate([product_0[None], product_1, product_2], axis=0)
    diag_cols = jnp.concatenate(
        [
            tile_cols(diag_full_0, c, tile)[None],
            lax.dynamic_slice_in_dim(diag_full_1, c * tile, tile, 2),
            diag_2,
        ],
        axis=0,
    )
    return ((-products)[None], diag_cols[None])


def solution(mesh):
    return jax.shard_map(
        body,
        mesh=mesh,
        in_specs=(
            P(("leaf", "row"), "col"),
            P("leaf", None, "row", "col"),
            P("leaf", None, "col", None),
            P("leaf", None, None),
            P("leaf", None),
        ),
        out_specs=(P("leaf", None, "row", "col"), P("leaf", None, None, "col")),
        check_vma=False,
    )
```

profile of v0, /device:TPU:0, one launch (start us, length us, event | category | flops | bytes accessed | tf_op | source)
XLA Modules:
  0.0 459.2 jit_solution(14943117877159287603)
XLA Ops:
  8.1 1.4 copy-done
  9.5 3.9 fusion.2
  14.3 57.6 %all-reduce.4.cloned.1.call-done = f32[7,128,512]{2,1,0:T(8,128)} async-done(((f32[7,128,512]{2,1,0:T(8,128)}), f32[7,128,512]{2,1,0:T(8,128)}) %all-reduce.4.cloned.1.call-update) | async-done | bytes 1835024 | tf_op jit(solution)/shard_map/psum | solution.py:57
  72.0 1.8 broadcast_multiply_fusion
  73.7 1.2 copy-done.2
  75.9 2.3 fusion
  78.3 18.1 %all-gather.10.cloned.1.call-done = f32[4096,256]{1,0:T(8,128)} async-done(((f32[32,256]{1,0:T(8,128)}), f32[4096,256]{1,0:T(8,128)}) %all-gather.10.cloned.1.call-update) | async-done | bytes 4194320 | tf_op jit(solution)/shard_map/all_gather | solution.py:67
  96.3 5.8 %copy.83 = f32[32,4,32,256]{3,1,2,0:T(4,128)S(1)} copy(f32[32,4,32,256]{3,2,1,0:T(8,128)} %bitcast.194) | data formatting | bytes 8388608 | tf_op jit(solution)/shard_map/reshape | solution.py:68
  102.2 3.0 copy.124
  105.1 20.2 %all-gather.8.cloned.1.call-done = f32[7,1024,128]{2,1,0:T(8,128)} async-done(((f32[7,128,128]{2,1,0:T(8,128)}), f32[7,1024,128]{2,1,0:T(8,128)}) %all-gather.8.cloned.1.call-update) | async-done | bytes 3670032 | tf_op jit(solution)/shard_map/all_gather | solution.py:62
  125.3 2.5 bitcast_dynamic-update-slice_fusion.6
  127.8 1.3 convolution_bitcast_fusion
  129.2 30.5 %reduce-scatter.4.cloned.1.call-done = f32[1,64,128]{2,1,0:T(8,128)} async-done(((f32[1,512,128]{2,1,0:T(8,128)}), f32[1,64,128]{2,1,0:T(8,128)}) %reduce-scatter.4.cloned.1.call-update) | async-done | bytes 32784 | tf_op jit(solution)/shard_map/reduce_scatter | solution.py:79
  170.4 3.1 fusion.102
  173.5 1.5 gather_fusion.1
  175.0 1.5 gather_fusion
  176.4 2.3 select_select_fusion.4
  179.7 2.3 constant_dynamic-slice_fusion.22
  182.0 23.9 %all-gather.12.cloned.1.call-done = f32[32,192,128]{2,1,0:T(8,128)} async-done(((f32[1,192,128]{2,1,0:T(8,128)}), f32[32,192,128]{2,1,0:T(8,128)}) %all-gather.12.cloned.1.call-update) | async-done | bytes 3145744 | tf_op jit(solution)/shard_map/all_gather | solution.py:84
  206.0 1.3 slice.190
  207.3 3.2 slice.189
  210.5 2.9 copy.114
  213.3 2.1 copy.133
  217.1 1.4 dynamic-slice_negate_fusion
  219.5 1.8 copy.117
  221.3 1.7 neg.74
  224.9 2.9 bitcast_dynamic-update-slice_fusion.5
  227.8 1.6 bitcast_dynamic-update-slice_fusion.4
  229.4 1.8 fusion.71
  231.2 30.5 %reduce-scatter.8.cloned.1.call-done = f32[2,64,128]{2,1,0:T(8,128)} async-done(((f32[2,512,128]{2,1,0:T(8,128)}), f32[2,64,128]{2,1,0:T(8,128)}) %reduce-scatter.8.cloned.1.call-update) | async-done | bytes 65552 | tf_op jit(solution)/shard_map/reduce_scatter | solution.py:79
  270.7 1.3 iota_reduce_fusion.3
  271.9 1.2 iota_reduce_fusion.2
  274.2 2.5 gather_fusion.7
  276.8 1.5 gather_fusion.9
  278.3 1.5 gather_fusion.5
  280.4 2.3 select_select_fusion.1
  285.9 1.9 copy.123
  287.8 2.1 copy.108
  290.8 1.7 gather_fusion.6
  293.7 1.3 gather_fusion.4
  299.2 12.6 %all-gather.14.cloned.1.call-done = f32[64,192,128]{2,1,0:T(8,128)} async-done(((f32[2,192,128]{2,1,0:T(8,128)}), f32[64,192,128]{2,1,0:T(8,128)}) %all-gather.14.cloned.1.call-update) | async-done | bytes 6291472 | tf_op jit(solution)/shard_map/all_gather | solution.py:84
  311.9 3.2 slice.195
  315.0 4.7 %slice.194 = f32[8,4,2,128,128]{4,3,2,1,0:T(8,128)} slice(f32[8,4,2,192,128]{4,3,2,1,0:T(8,128)} %bitcast.193), slice={[0:8], [0:4], [0:2], [0:128], [0:128]} | slice | bytes 8388608 | tf_op jit(solution)/shard_map/slice | solution.py:86
  319.8 5.3 %copy.118 = f32[8,4,2,128,128]{3,0,4,1,2:T(8,128)} copy(f32[8,4,2,128,128]{4,3,2,1,0:T(8,128)} %slice.194) | data formatting | bytes 8388608
  325.0 4.9 %reshape.293 = f32[2,1024,512]{1,2,0:T(8,128)} reshape(f32[2,8,128,4,128]{2,1,4,3,0:T(8,128)} %bitcast.183) | data formatting | bytes 8388608 | tf_op jit(solution)/shard_map/reshape | solution.py:86
  329.9 4.3 copy.134
  334.2 3.1 reshape.294
  337.3 4.2 select_bitcast_fusion.4
  345.8 7.9 %select_bitcast_fusion = (f32[1024,512]{0,1:T(8,128)}, f32[1,1024,512]{1,2,0:T(8,128)}, f32[1,1024,512]{1,2,0:T(8,128)}, f32[1,1024,512]{1,2,0:T(8,128)}) fusion(f32[2,1024,512]{1,2,0:T(8,128)} %reshape.293, s32[]{:T(128)S(6)} %select_n.346, pred[]{:T(512)S(6)} %and.78, s32[]{:T(128)S(6)} %select_n.326, s32[]{:T(128)S(6)} %select_n.316, s32[]{:T(128)S(6)} %select_n.336), kind=kLoop, calls=%fused_computation.12 | loop fusion | flops 524288 | bytes 16777232 | tf_op jit(solution)/shard_map/jit(_take)/select_n | solution.py:127
  353.6 2.9 copy.121
  356.6 1.9 select_bitcast_fusion.2
  360.5 1.9 negate_bitcast_fusion
  363.7 3.0 copy.119
  366.7 1.9 select_bitcast_fusion.3
  370.6 2.9 copy.122
  373.5 1.9 select_bitcast_fusion.1
  377.5 3.3 bitcast_dynamic-update-slice_fusion.3
  380.8 1.6 bitcast_dynamic-update-slice_fusion.2
  382.4 1.6 bitcast_dynamic-update-slice_fusion.1
  384.0 1.6 bitcast_dynamic-update-slice_fusion
  385.6 1.8 fusion.62
  390.2 1.2 constant_dynamic-slice_fusion.8
  391.4 57.6 %all-reduce.6.cloned.1.call-done = f32[4,512,128]{2,1,0:T(8,128)} async-done(((f32[4,512,128]{2,1,0:T(8,128)}), f32[4,512,128]{2,1,0:T(8,128)}) %all-reduce.6.cloned.1.call-update) | async-done | bytes 1048592 | tf_op jit(solution)/shard_map/psum | solution.py:157
  449.1 2.6 maximum_bitcast_fusion
  (185 shorter events, 42.8 us)
Async XLA Ops:
  8.0 1.5 copy-start
  8.0 6.0 %copy-start.37 = (s32[1,6,8]{2,0,1:T(1,128)S(1)}, s32[1,6,8]{2,0,1:T(1,128)}, u32[]{:S(2)}) copy-start(s32[1,6,8]{2,0,1:T(1,128)} %param.18) | copy-start | bytes 580
  8.0 63.9 %all-reduce.4.cloned.1.call-start = ((), (), s32[]{:S(2)}) async-start(), calls=%async_computation.3 | async-start | bytes 3670016 | tf_op jit(solution)/shard_map/psum | solution.py:57
  13.4 82.9 %all-gather.10.cloned.1.call-start = ((), (), s32[]{:S(2)}) async-start(), calls=%async_computation.9 | async-start | bytes 4227072 | tf_op jit(solution)/shard_map/all_gather | solution.py:67
  14.0 111.3 %all-gather.8.cloned.1.call-start = ((), (), s32[]{:S(2)}) async-start(), calls=%async_computation.4 | async-start | bytes 4128768 | tf_op jit(solution)/shard_map/all_gather | solution.py:62
  73.7 1.2 copy-start.2
  75.8 53.4 %reduce-scatter.6.cloned.1.call-start = ((), (), s32[]{:S(2)}) async-start(), calls=%async_computation.6 | async-start | bytes 1146880 | tf_op jit(solution)/shard_map/reduce_scatter | solution.py:65
  78.2 81.5 %reduce-scatter.4.cloned.1.call-start = ((), (), s32[]{:S(2)}) async-start(), calls=%async_computation.5 | async-start | bytes 294912 | tf_op jit(solution)/shard_map/reduce_scatter | solution.py:79
  102.1 25.6 %copy-start.3 = (f32[7,128,512]{2,1,0:T(8,128)S(1)}, f32[7,128,512]{2,1,0:T(8,128)}, u32[]{:S(2)}) copy-start(f32[7,128,512]{2,1,0:T(8,128)} %copy-done.2) | copy-start | bytes 5505028
  129.1 76.9 %all-gather.12.cloned.1.call-start = ((), (), s32[]{:S(2)}) async-start(), calls=%async_computation.10 | async-start | bytes 3244032 | tf_op jit(solution)/shard_map/all_gather | solution.py:84
  161.2 100.5 %reduce-scatter.8.cloned.1.call-start = ((), (), s32[]{:S(2)}) async-start(), calls=%async_computation.7 | async-start | bytes 589824 | tf_op jit(solution)/shard_map/reduce_scatter | solution.py:79
  176.4 2.3 copy-start.12
  216.2 2.3 copy-start.5
  223.8 4.0 copy-start.16
  223.8 4.0 copy-start.21
  223.8 4.0 copy-start.30
  229.4 34.2 %copy-start.38 = (s32[1,4]{1,0:T(1,128)S(1)}, s32[1,4]{1,0:T(1,128)}, u32[]{:S(2)}) copy-start(s32[1,4]{1,0:T(1,128)} %param.19) | copy-start | bytes 52
  229.4 47.4 %copy-start.7 = (f32[1,1024,128]{2,1,0:T(8,128)S(1)}, f32[1,1024,128]{2,1,0:T(8,128)}, u32[]{:S(2)}) copy-start(f32[1,1024,128]{2,1,0:T(8,128)} %get-tuple-element.69) | copy-start | bytes 1572868
  231.2 47.1 %copy-start.6 = (f32[1,1024,128]{2,1,0:T(8,128)S(1)}, f32[1,1024,128]{2,1,0:T(8,128)}, u32[]{:S(2)}) copy-start(f32[1,1024,128]{2,1,0:T(8,128)} %get-tuple-element.71) | copy-start | bytes 1572868
  231.2 80.7 %all-gather.14.cloned.1.call-start = ((), (), s32[]{:S(2)}) async-start(), calls=%async_computation.11 | async-start | bytes 6488064 | tf_op jit(solution)/shard_map/all_gather | solution.py:84
  263.3 185.8 %all-reduce.6.cloned.1.call-start = ((), (), s32[]{:S(2)}) async-start(), calls=%async_computation.8 | async-start | bytes 2097152 | tf_op jit(solution)/shard_map/psum | solution.py:157
  280.4 2.3 copy-start.11
  280.4 3.4 copy-start.10
  283.8 6.0 %copy-start.19 = (f32[1024,128]{0,1:T(8,128)S(1)}, f32[1024,128]{0,1:T(8,128)}, u32[]{:S(2)}) copy-start(f32[1024,128]{0,1:T(8,128)} %get-tuple-element.76) | copy-start | bytes 1572868
  285.9 7.6 %copy-start.18 = (f32[1024,128]{0,1:T(8,128)S(1)}, f32[1024,128]{0,1:T(8,128)}, u32[]{:S(2)}) copy-start(f32[1024,128]{0,1:T(8,128)} %get-tuple-element.77) | copy-start | bytes 1572868
  290.8 6.0 %copy-start.17 = (f32[1024,128]{0,1:T(8,128)S(1)}, f32[1024,128]{0,1:T(8,128)}, u32[]{:S(2)}) copy-start(f32[1024,128]{0,1:T(8,128)} %get-tuple-element.78) | copy-start | bytes 1572868
  293.7 4.9 %copy-start.22 = (f32[1024,128]{1,0:T(8,128)S(1)}, f32[1024,128]{1,0:T(8,128)}, u32[]{:S(2)}) copy-start(f32[1024,128]{1,0:T(8,128)} %copy.108) | copy-start | bytes 1572868
  356.6 2.7 copy-start.34
  359.3 4.1 copy-start.31
  366.7 2.7 copy-start.33
  373.5 2.7 copy-start.32
  377.4 3.4 copy-start.8
  377.4 3.4 copy-start.15
  377.4 3.4 copy-start.24
  377.4 3.4 copy-start.26
  377.4 3.4 copy-start.29
  377.4 5.0 %copy-start.9 = (f32[128,1536]{1,0:T(8,128)S(1)}, f32[128,1536]{1,0:T(8,128)}, u32[]{:S(2)}) copy-start(f32[128,1536]{1,0:T(8,128)} %copy.106) | copy-start | bytes 2359300
  377.4 5.0 %copy-start.14 = (f32[12,128,128]{2,1,0:T(8,128)S(1)}, f32[12,128,128]{2,1,0:T(8,128)}, u32[]{:S(2)}) copy-start(f32[12,128,128]{2,1,0:T(8,128)} %select_select_fusion.1) | copy-start | bytes 2359300
  377.4 5.0 %copy-start.23 = (f32[128,512]{1,0:T(8,128)S(1)}, f32[128,512]{1,0:T(8,128)}, u32[]{:S(2)}) copy-start(f32[128,512]{1,0:T(8,128)} %get-tuple-element.87) | copy-start | bytes 786436
  377.4 5.0 %copy-start.27 = (f32[128,512]{1,0:T(8,128)S(1)}, f32[128,512]{1,0:T(8,128)}, u32[]{:S(2)}) copy-start(f32[128,512]{1,0:T(8,128)} %dynamic-slice_negate_fusion.5) | copy-start | bytes 786436
  377.4 5.0 %copy-start.28 = (f32[128,512]{1,0:T(8,128)S(1)}, f32[128,512]{1,0:T(8,128)}, u32[]{:S(2)}) copy-start(f32[128,512]{1,0:T(8,128)} %copy.105) | copy-start | bytes 786436
  380.8 3.2 copy-start.13
  380.8 3.2 copy-start.20
  380.8 3.2 copy-start.25
  385.6 1.8 copy-start.36
  387.4 2.0 copy-start.35
  387.4 1.0 copy-start.4
  390.2 61.4 %copy-start.1 = (f32[1,7,128,512]{3,2,1,0:T(8,128)S(1)}, f32[1,7,128,512]{3,2,1,0:T(8,128)}, u32[]{:S(2)}) copy-start(f32[1,7,128,512]{3,2,1,0:T(8,128)} %param.17) | copy-start | bytes 5505028
Sparse Core Ops, SparseCore 0:
  13.5 58.3 all-reduce.3
  79.1 22.6 reduce-scatter.5
  129.2 30.4 reduce-scatter.3
  162.1 43.8 all-gather.11
  231.3 30.3 reduce-scatter.7
  263.8 48.0 all-gather.13
Sparse Core Ops, SparseCore 1:
  17.0 79.3 all-gather.9
  98.5 26.8 all-gather.7
  388.5 60.5 all-reduce.5
where the time goes:
time: 461 us; the launch traced here: 459 us
  waiting for transfers between devices  252 us (55%)
  local copies, waits for them, and re-layouts  100 us (22%)
  other arithmetic  53.9 us (12%)
  between operations  26.5 us (6%)
  matrix products  26 us (6%)
    reduce_scatter x2, waiting for transfers between devices, reduce_and_gather(): lax.psum_scatter(diag_partial(first, products), 'row', scatter_dimension=...  61 us
    psum x1, waiting for transfers between devices, body(): factor_rows = lax.psum(partial_factor, 'col')  57.6 us
    psum x1, waiting for transfers between devices, body(): diag_2 = lax.psum(diag_partial(first_2, product_2) + gram_rows, 'row')  57.6 us
    all_gather x2, waiting for transfers between devices, reduce_and_gather(): everything = lax.all_gather(both, ('row', 'col'), axis=0)  36.5 us
    unnamed x92, local copies, waits for them, and re-layouts  35.4 us
    dot_general x12, matrix products, mm(): jnp.matmul(a, b, precision=HIGHEST, preferred_element_type=jnp.float32)  26 us
    all_gather x1, waiting for transfers between devices, body(): factor_cols = lax.all_gather(factor_tile, 'row', axis=1, tiled=True)  20.2 us
    all_gather x1, waiting for transfers between devices, body(): gathered = lax.all_gather(sigma_top, ('leaf', 'row', 'col'), axis=0)  18.1 us
  transfers between devices with their start and end apart: 9, of which 8 were waited for; matrix products, arithmetic and copies ran while one was open for 15% of the time, Pallas kernels for 0%

commit v1 on v0

--- a/solution.py
+++ b/solution.py
@@ -54,7 +54,10 @@
     positions = slot_count + own_tiles
     band = width // row_count
     partial_factor = mm(panel, inverse)
-    factor_rows = lax.psum(partial_factor, "col")
+    dev_count = lax.axis_size("col")
+    factor_rows = partial_factor
+    for u in [[(s, s ^ rr) for s in range(dev_count)] for rr in (1, 2, 4, 8, 16) if rr < dev_count]:
+        factor_rows = factor_rows + lax.ppermute(factor_rows, "col", u)
     living = jnp.concatenate([jnp.ones((1, slot_count), jnp.bool_), picks_all >= 0], axis=0)
     live_here = jnp.take(living, r, axis=1).astype(jnp.float32)
     factor_rows = factor_rows * live_here[:, None, None]

time: 461 us -> 479 us (1.039)
  waiting for transfers between devices: 252 us -> 264 us
  starting transfers between devices: 0.77 us -> 5.7 us
    ppermute x0 -> x2, waiting for transfers between devices: none -> 86.2 us  [body(): factor_rows = factor_rows + lax.ppermute(factor_rows, 'col', u)]
    psum x1 -> x0, waiting for transfers between devices: 57.6 us -> none  [body(): factor_rows = lax.psum(partial_factor, 'col')]
    all_gather x1, waiting for transfers between devices: 18.1 us -> 0.02 us  [body(): gathered = lax.all_gather(sigma_top, ('leaf', 'row', 'col'), axis=0)]
    ppermute x0 -> x2, starting transfers between devices: none -> 4.96 us  [body(): factor_rows = factor_rows + lax.ppermute(factor_rows, 'col', u)]
  transfers between devices with their start and end apart: 9 -> 10, of which waited for: 8 -> 8; matrix products, arithmetic and copies ran while one was open for 15% -> 15% of each run, Pallas kernels for 0% -> 0%
where the time goes in v1:
time: 479 us; the launch traced here: 477 us
  waiting for transfers between devices  264 us (55%)
  local copies, waits for them, and re-layouts  99.6 us (21%)
  other arithmetic  56.3 us (12%)
  between operations  26.2 us (5%)
  matrix products  24.8 us (5%)
  starting transfers between devices  5.7 us (1%)
    ppermute x2, waiting for transfers between devices, body(): factor_rows = factor_rows + lax.ppermute(factor_rows, 'col', u)  86.2 us
    reduce_scatter x2, waiting for transfers between devices, reduce_and_gather(): lax.psum_scatter(diag_partial(first, products), 'row', scatter_dimension=...  60.7 us
    psum x1, waiting for transfers between devices, body(): diag_2 = lax.psum(diag_partial(first_2, product_2) + gram_rows, 'row')  57.8 us
    all_gather x2, waiting for transfers between devices, reduce_and_gather(): everything = lax.all_gather(both, ('row', 'col'), axis=0)  36.8 us
    unnamed x92, local copies, waits for them, and re-layouts  34.7 us
    dot_general x12, matrix products, mm(): jnp.matmul(a, b, precision=HIGHEST, preferred_element_type=jnp.float32)  24.8 us
    all_gather x1, waiting for transfers between devices, body(): factor_cols = lax.all_gather(factor_tile, 'row', axis=1, tiled=True)  22.1 us
    select_n x4, other arithmetic, body(): product_p = jnp.take(product_full_1, parent, axis=0)  13.4 us
  transfers between devices with their start and end apart: 10, of which 8 were waited for; matrix products, arithmetic and copies ran while one was open for 15% of the time, Pallas kernels for 0%

profile of v1, /device:TPU:0, one launch (start us, length us, event | category | flops | bytes accessed | tf_op | source)
XLA Modules:
  0.0 477.0 jit_solution(6994309933131596920)
XLA Ops:
  9.5 2.6 fusion.2
  12.2 1.7 collective-permute-start
  13.8 41.4 %collective-permute-done = f32[7,128,512]{2,1,0:T(8,128)S(1)} collective-permute-done((f32[7,128,512]{2,1,0:T(8,128)S(1)}, f32[7,128,512]{2,1,0:T(8,128)S(1)}, u32[]{:S(2)}, u32[]{:S(2)}) %collective-permute-start) | collective-permute-done | bytes 1835040 | tf_op jit(solution)/shard_map/ppermute | solution.py:60
  55.3 1.6 add.120
  56.9 3.3 collective-permute-start.1
  60.5 44.7 %collective-permute-done.1 = f32[7,128,512]{2,1,0:T(8,128)} collective-permute-done((f32[7,128,512]{2,1,0:T(8,128)}, f32[7,128,512]{2,1,0:T(8,128)}, u32[]{:S(2)}, u32[]{:S(2)}) %collective-permute-start.1) | collective-permute-done | bytes 1835040 | tf_op jit(solution)/shard_map/ppermute | solution.py:60
  105.2 2.6 add_multiply_fusion
  107.8 1.2 copy-done.2
  109.9 2.3 fusion
  112.4 5.8 %copy.83 = f32[32,4,32,256]{3,1,2,0:T(4,128)S(1)} copy(f32[32,4,32,256]{3,2,1,0:T(8,128)} %bitcast.194) | data formatting | bytes 8388608 | tf_op jit(solution)/shard_map/reshape | solution.py:71
  118.2 3.0 copy.124
  121.1 22.1 %all-gather.8.cloned.1.call-done = f32[7,1024,128]{2,1,0:T(8,128)} async-done(((f32[7,128,128]{2,1,0:T(8,128)}), f32[7,1024,128]{2,1,0:T(8,128)}) %all-gather.8.cloned.1.call-update) | async-done | bytes 3670032 | tf_op jit(solution)/shard_map/all_gather | solution.py:65
  143.2 2.5 bitcast_dynamic-update-slice_fusion.6
  145.7 1.3 convolution_bitcast_fusion
  147.1 30.4 %reduce-scatter.4.cloned.1.call-done = f32[1,64,128]{2,1,0:T(8,128)} async-done(((f32[1,512,128]{2,1,0:T(8,128)}), f32[1,64,128]{2,1,0:T(8,128)}) %reduce-scatter.4.cloned.1.call-update) | async-done | bytes 32784 | tf_op jit(solution)/shard_map/reduce_scatter | solution.py:82
  188.2 2.3 constant_dynamic-slice_fusion.22
  190.5 3.1 fusion.102
  193.5 1.5 gather_fusion.1
  195.0 1.5 gather_fusion
  196.5 2.3 select_select_fusion.4
  199.8 24.1 %all-gather.12.cloned.1.call-done = f32[32,192,128]{2,1,0:T(8,128)} async-done(((f32[1,192,128]{2,1,0:T(8,128)}), f32[32,192,128]{2,1,0:T(8,128)}) %all-gather.12.cloned.1.call-update) | async-done | bytes 3145744 | tf_op jit(solution)/shard_map/all_gather | solution.py:87
  223.9 1.3 slice.190
  225.2 3.2 slice.189
  228.3 2.9 copy.114
  231.2 2.1 copy.133
  235.0 1.4 dynamic-slice_negate_fusion
  237.4 1.8 copy.117
  239.2 1.7 neg.74
  242.8 2.9 bitcast_dynamic-update-slice_fusion.5
  245.7 1.6 bitcast_dynamic-update-slice_fusion.4
  247.3 1.8 fusion.71
  249.1 30.3 %reduce-scatter.8.cloned.1.call-done = f32[2,64,128]{2,1,0:T(8,128)} async-done(((f32[2,512,128]{2,1,0:T(8,128)}), f32[2,64,128]{2,1,0:T(8,128)}) %reduce-scatter.8.cloned.1.call-update) | async-done | bytes 65552 | tf_op jit(solution)/shard_map/reduce_scatter | solution.py:82
  288.5 1.3 iota_reduce_fusion.3
  292.0 2.5 gather_fusion.7
  294.5 1.5 gather_fusion.9
  296.1 1.5 gather_fusion.5
  298.2 2.3 select_select_fusion.1
  303.7 1.9 copy.123
  305.5 2.1 copy.108
  308.6 1.7 gather_fusion.6
  311.5 1.3 gather_fusion.4
  317.0 12.7 %all-gather.14.cloned.1.call-done = f32[64,192,128]{2,1,0:T(8,128)} async-done(((f32[2,192,128]{2,1,0:T(8,128)}), f32[64,192,128]{2,1,0:T(8,128)}) %all-gather.14.cloned.1.call-update) | async-done | bytes 6291472 | tf_op jit(solution)/shard_map/all_gather | solution.py:87
  329.7 3.2 slice.195
  332.9 4.7 slice.194
  337.6 5.3 %copy.118 = f32[8,4,2,128,128]{3,0,4,1,2:T(8,128)} copy(f32[8,4,2,128,128]{4,3,2,1,0:T(8,128)} %slice.194) | data formatting | bytes 8388608
  342.9 4.9 %reshape.293 = f32[2,1024,512]{1,2,0:T(8,128)} reshape(f32[2,8,128,4,128]{2,1,4,3,0:T(8,128)} %bitcast.183) | data formatting | bytes 8388608 | tf_op jit(solution)/shard_map/reshape | solution.py:89
  347.7 4.3 copy.134
  352.1 3.1 reshape.294
  355.2 4.2 select_bitcast_fusion.4
  363.6 7.9 %select_bitcast_fusion = (f32[1024,512]{0,1:T(8,128)}, f32[1,1024,512]{1,2,0:T(8,128)}, f32[1,1024,512]{1,2,0:T(8,128)}, f32[1,1024,512]{1,2,0:T(8,128)}) fusion(f32[2,1024,512]{1,2,0:T(8,128)} %reshape.293, s32[]{:T(128)S(6)} %select_n.346, pred[]{:T(512)S(6)} %and.78, s32[]{:T(128)S(6)} %select_n.326, s32[]{:T(128)S(6)} %select_n.316, s32[]{:T(128)S(6)} %select_n.336), kind=kLoop, calls=%fused_computation.12 | loop fusion | flops 524288 | bytes 16777232 | tf_op jit(solution)/shard_map/jit(_take)/select_n | solution.py:130
  371.5 2.9 copy.121
  374.4 1.9 select_bitcast_fusion.2
  378.4 1.9 negate_bitcast_fusion
  381.6 3.0 copy.119
  384.5 1.9 select_bitcast_fusion.3
  388.4 2.9 copy.122
  391.4 1.9 select_bitcast_fusion.1
  395.3 3.3 bitcast_dynamic-update-slice_fusion.3
  398.7 1.6 bitcast_dynamic-update-slice_fusion.2
  400.3 1.6 bitcast_dynamic-update-slice_fusion.1
  401.9 1.6 bitcast_dynamic-update-slice_fusion
  403.4 1.8 fusion.62
  409.3 57.8 %all-reduce.3.cloned.1.call-done = f32[4,512,128]{2,1,0:T(8,128)} async-done(((f32[4,512,128]{2,1,0:T(8,128)}), f32[4,512,128]{2,1,0:T(8,128)}) %all-reduce.3.cloned.1.call-update) | async-done | bytes 1048592 | tf_op jit(solution)/shard_map/psum | solution.py:160
  467.1 2.6 maximum_bitcast_fusion
  (187 shorter events, 46.1 us)
Async XLA Ops:
  8.0 1.5 copy-start
  8.0 104.3 %all-gather.10.cloned.1.call-start = ((), (), s32[]{:S(2)}) async-start(), calls=%async_computation.8 | async-start | bytes 4227072 | tf_op jit(solution)/shard_map/all_gather | solution.py:70
  8.7 134.5 %all-gather.8.cloned.1.call-start = ((), (), s32[]{:S(2)}) async-start(), calls=%async_computation.3 | async-start | bytes 4128768 | tf_op jit(solution)/shard_map/all_gather | solution.py:65
  12.2 48.1 %copy-start.37 = (s32[1,6,8]{2,0,1:T(1,128)S(1)}, s32[1,6,8]{2,0,1:T(1,128)}, u32[]{:S(2)}) copy-start(s32[1,6,8]{2,0,1:T(1,128)} %param.18) | copy-start | bytes 580
  12.2 43.1 %collective-permute-start = (f32[7,128,512]{2,1,0:T(8,128)S(1)}, f32[7,128,512]{2,1,0:T(8,128)S(1)}, u32[]{:S(2)}, u32[]{:S(2)}) collective-permute-start(f32[7,128,512]{2,1,0:T(8,128)S(1)} %fusion.2), channel_id=1, source_target_pairs={{0,1},{1,0},{2,3},{3,2},{4,5},{5,4},{6,7},{7,6},{8,9},{9,8},{10,11... | collective-permute-start | bytes 5505032 | tf_op jit(solution)/shard_map/ppermute | solution.py:60
  56.9 48.3 %collective-permute-start.1 = (f32[7,128,512]{2,1,0:T(8,128)}, f32[7,128,512]{2,1,0:T(8,128)}, u32[]{:S(2)}, u32[]{:S(2)}) collective-permute-start(f32[7,128,512]{2,1,0:T(8,128)} %add.120), channel_id=1, source_target_pairs={{0,2},{1,3},{2,0},{3,1},{4,6},{5,7},{6,4},{7,5},{8,10},{9,11},{10,... | collective-permute-start | bytes 5505032 | tf_op jit(solution)/shard_map/ppermute | solution.py:60
  107.8 1.2 copy-start.2
  109.9 37.2 %reduce-scatter.6.cloned.1.call-start = ((), (), s32[]{:S(2)}) async-start(), calls=%async_computation.5 | async-start | bytes 1146880 | tf_op jit(solution)/shard_map/reduce_scatter | solution.py:68
  112.3 65.2 %reduce-scatter.4.cloned.1.call-start = ((), (), s32[]{:S(2)}) async-start(), calls=%async_computation.4 | async-start | bytes 294912 | tf_op jit(solution)/shard_map/reduce_scatter | solution.py:82
  118.1 27.6 %copy-start.3 = (f32[7,128,512]{2,1,0:T(8,128)S(1)}, f32[7,128,512]{2,1,0:T(8,128)}, u32[]{:S(2)}) copy-start(f32[7,128,512]{2,1,0:T(8,128)} %copy-done.2) | copy-start | bytes 5505028
  147.0 76.8 %all-gather.12.cloned.1.call-start = ((), (), s32[]{:S(2)}) async-start(), calls=%async_computation.9 | async-start | bytes 3244032 | tf_op jit(solution)/shard_map/all_gather | solution.py:87
  179.0 100.5 %reduce-scatter.8.cloned.1.call-start = ((), (), s32[]{:S(2)}) async-start(), calls=%async_computation.6 | async-start | bytes 589824 | tf_op jit(solution)/shard_map/reduce_scatter | solution.py:82
  196.5 2.3 copy-start.12
  234.1 2.3 copy-start.5
  241.7 4.0 copy-start.16
  241.7 4.0 copy-start.20
  241.7 4.0 copy-start.30
  247.3 34.1 %copy-start.38 = (s32[1,4]{1,0:T(1,128)S(1)}, s32[1,4]{1,0:T(1,128)}, u32[]{:S(2)}) copy-start(s32[1,4]{1,0:T(1,128)} %param.19) | copy-start | bytes 52
  247.3 47.3 %copy-start.7 = (f32[1,1024,128]{2,1,0:T(8,128)S(1)}, f32[1,1024,128]{2,1,0:T(8,128)}, u32[]{:S(2)}) copy-start(f32[1,1024,128]{2,1,0:T(8,128)} %get-tuple-element.69) | copy-start | bytes 1572868
  249.1 47.0 %copy-start.6 = (f32[1,1024,128]{2,1,0:T(8,128)S(1)}, f32[1,1024,128]{2,1,0:T(8,128)}, u32[]{:S(2)}) copy-start(f32[1,1024,128]{2,1,0:T(8,128)} %get-tuple-element.71) | copy-start | bytes 1572868
  249.1 80.6 %all-gather.14.cloned.1.call-start = ((), (), s32[]{:S(2)}) async-start(), calls=%async_computation.10 | async-start | bytes 6488064 | tf_op jit(solution)/shard_map/all_gather | solution.py:87
  281.1 186.0 %all-reduce.3.cloned.1.call-start = ((), (), s32[]{:S(2)}) async-start(), calls=%async_computation.7 | async-start | bytes 2097152 | tf_op jit(solution)/shard_map/psum | solution.py:160
  298.1 2.3 copy-start.11
  298.2 3.4 copy-start.10
  301.6 6.0 %copy-start.19 = (f32[1024,128]{0,1:T(8,128)S(1)}, f32[1024,128]{0,1:T(8,128)}, u32[]{:S(2)}) copy-start(f32[1024,128]{0,1:T(8,128)} %get-tuple-element.76) | copy-start | bytes 1572868
  303.7 7.6 %copy-start.18 = (f32[1024,128]{0,1:T(8,128)S(1)}, f32[1024,128]{0,1:T(8,128)}, u32[]{:S(2)}) copy-start(f32[1024,128]{0,1:T(8,128)} %get-tuple-element.77) | copy-start | bytes 1572868
  308.6 6.0 %copy-start.17 = (f32[1024,128]{0,1:T(8,128)S(1)}, f32[1024,128]{0,1:T(8,128)}, u32[]{:S(2)}) copy-start(f32[1024,128]{0,1:T(8,128)} %get-tuple-element.78) | copy-start | bytes 1572868
  311.4 4.9 %copy-start.22 = (f32[1024,128]{1,0:T(8,128)S(1)}, f32[1024,128]{1,0:T(8,128)}, u32[]{:S(2)}) copy-start(f32[1024,128]{1,0:T(8,128)} %copy.108) | copy-start | bytes 1572868
  374.4 2.7 copy-start.34
  377.1 4.1 copy-start.31
  384.5 2.7 copy-start.33
  391.4 2.7 copy-start.32
  395.2 3.4 copy-start.8
  395.2 3.4 copy-start.15
  395.2 3.4 copy-start.24
  395.2 3.4 copy-start.26
  395.3 3.4 copy-start.29
  395.3 5.0 %copy-start.9 = (f32[128,1536]{1,0:T(8,128)S(1)}, f32[128,1536]{1,0:T(8,128)}, u32[]{:S(2)}) copy-start(f32[128,1536]{1,0:T(8,128)} %copy.106) | copy-start | bytes 2359300
  395.3 5.0 %copy-start.14 = (f32[12,128,128]{2,1,0:T(8,128)S(1)}, f32[12,128,128]{2,1,0:T(8,128)}, u32[]{:S(2)}) copy-start(f32[12,128,128]{2,1,0:T(8,128)} %select_select_fusion.1) | copy-start | bytes 2359300
  395.3 5.0 %copy-start.23 = (f32[128,512]{1,0:T(8,128)S(1)}, f32[128,512]{1,0:T(8,128)}, u32[]{:S(2)}) copy-start(f32[128,512]{1,0:T(8,128)} %get-tuple-element.87) | copy-start | bytes 786436
  395.3 5.0 %copy-start.27 = (f32[128,512]{1,0:T(8,128)S(1)}, f32[128,512]{1,0:T(8,128)}, u32[]{:S(2)}) copy-start(f32[128,512]{1,0:T(8,128)} %dynamic-slice_negate_fusion.5) | copy-start | bytes 786436
  395.3 5.0 %copy-start.28 = (f32[128,512]{1,0:T(8,128)S(1)}, f32[128,512]{1,0:T(8,128)}, u32[]{:S(2)}) copy-start(f32[128,512]{1,0:T(8,128)} %copy.105) | copy-start | bytes 786436
  398.7 3.2 copy-start.13
  398.7 3.2 copy-start.21
  398.7 3.2 copy-start.25
  403.4 1.8 copy-start.36
  405.2 2.0 copy-start.35
  405.3 1.0 copy-start.4
  408.1 61.6 %copy-start.1 = (f32[1,7,128,512]{3,2,1,0:T(8,128)S(1)}, f32[1,7,128,512]{3,2,1,0:T(8,128)}, u32[]{:S(2)}) copy-start(f32[1,7,128,512]{3,2,1,0:T(8,128)} %param.17) | copy-start | bytes 5505028
Sparse Core Ops, SparseCore 0:
  12.0 71.4 all-gather.9
  110.0 33.1 all-gather.7
  406.4 60.6 all-reduce.2
Sparse Core Ops, SparseCore 1:
  112.8 25.9 reduce-scatter.5
  147.1 30.4 reduce-scatter.3
  179.9 43.9 all-gather.11
  249.2 30.2 reduce-scatter.7
  281.8 47.9 all-gather.13
